TPU v7x, 32 devices: a whole 2x2x4 slice. The times are simulated.
32 devices in a mesh: date: 2 (over x), strip: 16 (over z, y, core).
Axes of the slice: x: 2, y: 2, z: 4, core: 2. Of those that a mesh axis runs over, the one named last changes fastest.
Arguments:
- slc: bfloat16 [20, 2, 192, 1408], P('date', None, 'strip'), may hold values from -60 to 60
Outputs:
- coherence: float32 [20, 20, 2, 64, 128], P('date', None, None, 'strip')
All inputs are finite; a program needn't handle non-finite values.
Results may differ from a plain program's by a relative error of at most 0.0003.
Values may be sent and summed in bfloat16 or wider, within the bound.
No kernel may reach another device: no remote copies, remote signals or barrier semaphores. Data moves between devices by JAX's collectives and lax.ppermute only.
A program may use at most 128 MiB of HBM per device.

v0:
```python
import jax
import jax.numpy as jnp
from jax import lax
from jax.sharding import PartitionSpec as P

EPS = 1e-06


def with_halo(cells, sides, width):
    for axis, dim in sides:
        count = lax.axis_size(axis)
        ends = count - 1
        head = lax.slice_in_dim(cells, 0, width, axis=dim)
        tail = lax.slice_in_dim(cells, cells.shape[dim] - width, cells.shape[dim], axis=dim)
        cells = jnp.concatenate(
            [
                lax.ppermute(tail, axis, [(i, (i + 1) % count) for i in range(ends)]),
                cells,
                lax.ppermute(head, axis, [((i + 1) % count, i) for i in range(ends)]),
            ],
            axis=dim,
        )
    return cells


def cell_layout(block):
    shape = block.shape
    return block.reshape((shape[0], 2, shape[2] // 3, 3, shape[3] // 11, 11))


def boxcar(cells):
    padded = jnp.pad(cells, [(0, 0)] * (cells.ndim - 1) + [(1, 1)])
    tri = padded[..., :-2] + padded[..., 1:-1] + padded[..., 2:]
    return tri[..., :-2, :] + tri[..., 1:-1, :] + tri[..., 2:, :]


def amplitude(cells_bf):
    values = cells_bf.astype(jnp.float32)
    power = jnp.sum(values * values, axis=(1, 3, 5))
    return lax.rsqrt(boxcar(power) + EPS)


def pair_terms(own_cells, own_scale, other_cells, other_scale):
    sums = lax.dot_general(
        own_cells,
        other_cells,
        (((3, 5), (3, 5)), ((2, 4), (2, 4))),
        preferred_element_type=jnp.float32,
    )
    first = sums[:, :, :, 0, :, 0] + sums[:, :, :, 1, :, 1]
    second = sums[:, :, :, 1, :, 0] - sums[:, :, :, 0, :, 1]
    both = jnp.stack([first, second], axis=4)
    both = jnp.transpose(both, (2, 3, 4, 0, 1))
    return boxcar(both) * (own_scale[:, None] * other_scale[None])[:, :, None]


def per_device(slc):
    local_dates = slc.shape[0]
    whole = lax.all_gather(slc, "date", axis=0, tiled=True)
    padded = with_halo(whole, (("strip", 2),), 3)
    all_cells = cell_layout(padded)
    all_scale = amplitude(all_cells)
    first_date = lax.axis_index("date") * local_dates
    own_cells = lax.dynamic_slice_in_dim(all_cells, first_date, local_dates, 0)
    own_scale = lax.dynamic_slice_in_dim(all_scale, first_date, local_dates, 0)
    return pair_terms(own_cells, own_scale, all_cells, all_scale)


def solution(mesh):
    return jax.shard_map(
        per_device,
        mesh=mesh,
        in_specs=(P("date", None, "strip", None),),
        out_specs=P("date", None, None, "strip", None),
        check_vma=False,
    )
```

profile of v0, /device:TPU:5, one launch (start us, length us, event | category | flops | bytes accessed | tf_op | source)
XLA Modules:
  0.0 243.3 jit_solution(3144084779581970662)
XLA Ops:
  6.5 0.7 all-gather.2.cloned.1.call-update
  7.3 27.6 %all-gather.2.cloned.1.call-done = bf16[20,2,12,1408]{3,1,2,0:T(2,128)(2,1)} async-done(((bf16[10,2,12,1408]{3,1,2,0:T(2,128)(2,1)}), bf16[20,2,12,1408]{3,1,2,0:T(2,128)(2,1)}) %all-gather.2.cloned.1.call-update) | async-done | bytes 1351696 | tf_op jit(solution)/shard_map/all_gather | solution.py:59
  34.9 1.7 fusion.14
  36.5 3.7 %collective-permute-start = (bf16[20,2,3,1408]{3,1,2,0:T(2,128)(2,1)S(1)}, bf16[20,2,3,1408]{3,1,2,0:T(2,128)(2,1)S(1)}, u32[]{:S(2)}, u32[]{:S(2)}) collective-permute-start(bf16[20,2,3,1408]{3,1,2,0:T(2,128)(2,1)S(1)} %get-tuple-element.8), channel_id=1, source_target_pairs={{0,1},{1,2},{2,3},{3,4},{4,5},{5,6},{6,7},{7,8},{8,9},{9,10},{10,1... | collective-permute-start | bytes 1013768 | tf_op jit(solution)/shard_map/ppermute | solution.py:17
  40.2 1.9 collective-permute-start.1
  42.1 2.2 collective-permute-done
  44.5 1.1 constant_dynamic-update-slice_fusion.1
  45.6 4.0 %collective-permute-done.1 = bf16[20,2,3,1408]{3,1,2,0:T(2,128)(2,1)S(1)} collective-permute-done((bf16[20,2,3,1408]{3,1,2,0:T(2,128)(2,1)S(1)}, bf16[20,2,3,1408]{3,1,2,0:T(2,128)(2,1)S(1)}, u32[]{:S(2)}, u32[]{:S(2)}) %collective-permute-start.1) | collective-permute-done | bytes 337952 | tf_op jit(solution)/shard_map/ppermute | solution.py:19
  49.6 0.3 constant_dynamic-update-slice_fusion
  49.9 1.3 copy-done
  51.2 5.4 %multiply_reduce_fusion = f32[20,18,1408]{2,1,0:T(8,128)S(1)} fusion(bf16[20,2,18,1408]{3,1,2,0:T(2,128)(2,1)S(1)} %constant_dynamic-update-slice_fusion), kind=kLoop, calls=%fused_computation.8 | loop fusion | flops 2534400 | bytes 4055040 | tf_op jit(solution)/shard_map/reduce_sum | solution.py:39
  56.6 55.1 %reshape.43 = bf16[20,2,6,3,128,11]{5,4,1,3,2,0:T(8,128)(2,1)} reshape(bf16[20,2,18,1408]{3,1,2,0:T(2,128)(2,1)} %copy-done) | data formatting | bytes 4055040 | tf_op jit(solution)/shard_map/reshape | solution.py:28
  111.7 1.8 copy.15
  113.5 26.9 %reduce_sum.14 = f32[20,6,3,128,11]{4,3,0,2,1:T(8,128)} reshape(f32[20,18,1408]{2,0,1:T(8,128)} %copy.15) | data formatting | bytes 4055040 | tf_op jit(solution)/shard_map/reduce_sum | solution.py:39
  140.4 9.3 %reduce_sum.18 = f32[20,6,128]{2,0,1:T(8,128)S(1)} reduce(f32[20,6,3,128,11]{4,3,0,2,1:T(8,128)} %reduce_sum.14, f32[]{:T(128)} %constant.15.clone.1), dimensions={2,4}, to_apply=%region_1.2 | reduce | flops 491520 | bytes 2088964 | tf_op jit(solution)/shard_map/reduce_sum | solution.py:39
  149.9 11.3 %constant_dynamic-slice_fusion.1 = bf16[10,2,6,3,128,11]{5,4,1,3,2,0:T(8,128)(2,1)} fusion(bf16[20,2,6,3,128,11]{5,4,1,3,2,0:T(8,128)(2,1)} %reshape.43, s32[]{:T(128)S(6)} %select_n.4), kind=kLoop, calls=%fused_computation.30 | loop fusion | bytes 2027524 | tf_op jit(solution)/shard_map/dynamic_slice | solution.py:64
  161.2 45.5 %fusion.2 = f32[6,128,10,2,20,2]{4,2,5,3,1,0:T(8,128)} fusion(bf16[20,2,6,3,128,11,1]{5,4,1,3,2,0,6:T(8,128)(2,1)} %bitcast.21, bf16[10,2,6,3,128,11]{5,4,1,3,2,0:T(8,128)(2,1)} %constant_dynamic-slice_fusion.1), kind=kOutput, calls=%fused_computation.3 | convolution fusion | flops 40550400 | bytes 5498880 | tf_op jit(solution)/shard_map/dot_general | solution.py:44
  206.7 14.2 %fusion.6 = (f32[6,128,10,20,1]{3,2,1,0,4:T(8,128)}, f32[6,128,10,20,1]{3,2,1,0,4:T(8,128)}) fusion(f32[6,128,10,2,20,2]{4,2,5,3,1,0:T(8,128)} %fusion.2), kind=kLoop, calls=%fused_computation.7 | loop fusion | flops 307200 | bytes 3686400 | tf_op jit(solution)/shard_map/add | solution.py:50
  220.8 5.0 %copy.13 = f32[6,128,10,20,1]{1,4,3,2,0:T(1,128)S(1)} copy(f32[6,128,10,20,1]{3,2,1,0,4:T(8,128)} %get-tuple-element.5) | data formatting | bytes 1228800 | tf_op jit(solution)/shard_map/add | solution.py:50
  225.8 5.2 %copy.14 = f32[6,128,10,20,1]{1,4,3,2,0:T(1,128)S(1)} copy(f32[6,128,10,20,1]{3,2,1,0,4:T(8,128)} %get-tuple-element.6) | data formatting | bytes 1228800 | tf_op jit(solution)/shard_map/sub | solution.py:51
  231.0 1.1 maximum_bitcast_fusion
  232.1 2.6 %fusion.8 = f32[10,20,2,6,128]{4,2,1,0,3:T(2,128)S(1)} fusion(f32[10,20,2,6,128]{4,2,1,0,3:T(2,128)S(1)} %maximum_bitcast_fusion), kind=kLoop, calls=%fused_computation.12 | loop fusion | flops 614400 | bytes 2457600 | tf_op jit(solution)/shard_map/add | solution.py:33
  234.7 0.5 fusion.9
  235.3 1.2 copy.16
  (9 shorter events, 0.4 us)
Async XLA Ops:
  6.5 28.3 %all-gather.2.cloned.1.call-start = ((), (), s32[]{:S(2)}) async-start(), calls=%async_computation | async-start | bytes 2027520 | tf_op jit(solution)/shard_map/all_gather | solution.py:59
  34.9 9.7 %copy-start.1 = (bf16[20,2,12,1408]{3,1,2,0:T(2,128)(2,1)S(1)}, bf16[20,2,12,1408]{3,1,2,0:T(2,128)(2,1)}, u32[]{:S(2)}) copy-start(bf16[20,2,12,1408]{3,1,2,0:T(2,128)(2,1)} %all-gather.2.cloned.1.call-done) | copy-start | bytes 4055044
  36.5 7.8 %collective-permute-start = (bf16[20,2,3,1408]{3,1,2,0:T(2,128)(2,1)S(1)}, bf16[20,2,3,1408]{3,1,2,0:T(2,128)(2,1)S(1)}, u32[]{:S(2)}, u32[]{:S(2)}) collective-permute-start(bf16[20,2,3,1408]{3,1,2,0:T(2,128)(2,1)S(1)} %get-tuple-element.8), channel_id=1, source_target_pairs={{0,1},{1,2},{2,3},{3,4},{4,5},{5,6},{6,7},{7,8},{8,9},{9,10},{10,1... | collective-permute-start | bytes 1013768 | tf_op jit(solution)/shard_map/ppermute | solution.py:17
  40.2 9.4 %collective-permute-start.1 = (bf16[20,2,3,1408]{3,1,2,0:T(2,128)(2,1)S(1)}, bf16[20,2,3,1408]{3,1,2,0:T(2,128)(2,1)S(1)}, u32[]{:S(2)}, u32[]{:S(2)}) collective-permute-start(bf16[20,2,3,1408]{3,1,2,0:T(2,128)(2,1)S(1)} %get-tuple-element.7), channel_id=1, source_target_pairs={{1,0},{2,1},{3,2},{4,3},{5,4},{6,5},{7,6},{8,7},{9,8},{10,9},{11,1... | collective-permute-start | bytes 1013768 | tf_op jit(solution)/shard_map/ppermute | solution.py:19
  49.9 1.3 copy-start
Sparse Core Ops, SparseCore 0:
  8.9 25.9 all-gather.1
where the time goes:
time: 244 us; the launch traced here: 243 us
  local copies, waits for them, and re-layouts  111 us (45%)
  matrix products  45.5 us (19%)
  waiting for transfers between devices  34.5 us (14%)
  other arithmetic  33.2 us (14%)
  between operations  13.5 us (6%)
  starting transfers between devices  5.59 us (2%)
    reshape x1, local copies, waits for them, and re-layouts, cell_layout(): return block.reshape((shape[0], 2, shape[2] // 3, 3, shape[3] // 11, 11))  55.1 us
    dot_general x1, matrix products, pair_terms(): lax.dot_general(own_cells, other_cells, (((3, 5), (3, 5)), ((2, 4), (2, 4...  45.5 us
    reduce_sum x2, local copies, waits for them, and re-layouts, amplitude(): power = jnp.sum(values * values, axis=(1, 3, 5))  28.7 us
    all_gather x1, waiting for transfers between devices, per_device(): whole = lax.all_gather(slc, 'date', axis=0, tiled=True)  27.6 us
    reduce_sum x2, other arithmetic, amplitude(): power = jnp.sum(values * values, axis=(1, 3, 5))  14.7 us
    add x1, other arithmetic, pair_terms(): first = sums[:, :, :, 0, :, 0] + sums[:, :, :, 1, :, 1]  14.2 us
    dynamic_slice x1, local copies, waits for them, and re-layouts, per_device(): own_cells = lax.dynamic_slice_in_dim(all_cells, first_date, local_dates, 0)  11.3 us
    sub x1, local copies, waits for them, and re-layouts, pair_terms(): second = sums[:, :, :, 1, :, 0] - sums[:, :, :, 0, :, 1]  5.2 us
  transfers between devices with their start and end apart: 3, of which 3 were waited for; matrix products, arithmetic and copies ran while one was open for 1% of the time, Pallas kernels for 0%

commit v1 on v0

--- a/solution.py
+++ b/solution.py
@@ -56,7 +56,15 @@
 
 def per_device(slc):
     local_dates = slc.shape[0]
-    whole = lax.all_gather(slc, "date", axis=0, tiled=True)
+    ways, here, step = (lax.axis_size("date"), lax.axis_index("date"), slc.shape[0])
+    line, have = (slc, 1)
+    while have < ways:
+        line = jnp.concatenate(
+            [line, lax.ppermute(line, "date", [(d, (d - have) % ways) for d in range(ways)])],
+            axis=0,
+        )
+        have = 2 * have
+    whole = jnp.roll(line, here * step, axis=0)
     padded = with_halo(whole, (("strip", 2),), 3)
     all_cells = cell_layout(padded)
     all_scale = amplitude(all_cells)

time: 244 us -> 221 us (0.906)
  between operations: 13.5 us -> 0.13 us
  waiting for transfers between devices: 34.5 us -> 22.5 us
  other arithmetic: 33.2 us -> 41.3 us
  local copies, waits for them, and re-layouts: 111 us -> 104 us
    all_gather x1 -> x0, waiting for transfers between devices: 27.6 us -> none  [per_device(): whole = lax.all_gather(slc, 'date', axis=0, tiled=True)]
    ppermute x0 -> x1, waiting for transfers between devices: none -> 15 us  [per_device(): lax.ppermute(line, 'date', [(d, (d - have) % ways) for d in range(ways)])]
    concatenate x0 -> x1, other arithmetic: none -> 6.57 us  [per_device(): whole = jnp.roll(line, here * step, axis=0)]
    unnamed x6 -> x2, local copies, waits for them, and re-layouts: 2.63 us -> 0.01 us
  transfers between devices with their start and end apart: 3 -> 3, of which waited for: 3 -> 3; matrix products, arithmetic and copies ran while one was open for 1% -> 0% of each run, Pallas kernels for 0% -> 0%
where the time goes in v1:
time: 221 us
  local copies, waits for them, and re-layouts  104 us (47%)
  matrix products  45.5 us (21%)
  other arithmetic  41.3 us (19%)
  waiting for transfers between devices  22.5 us (10%)
  starting transfers between devices  7.71 us (3%)
    reshape x1, local copies, waits for them, and re-layouts, cell_layout(): return block.reshape((shape[0], 2, shape[2] // 3, 3, shape[3] // 11, 11))  54 us
    dot_general x1, matrix products, pair_terms(): lax.dot_general(own_cells, other_cells, (((3, 5), (3, 5)), ((2, 4), (2, 4...  45.5 us
    reduce_sum x2, local copies, waits for them, and re-layouts, amplitude(): power = jnp.sum(values * values, axis=(1, 3, 5))  26.4 us
    reduce_sum x2, other arithmetic, amplitude(): power = jnp.sum(values * values, axis=(1, 3, 5))  16.2 us
    ppermute x1, waiting for transfers between devices, per_device(): lax.ppermute(line, 'date', [(d, (d - have) % ways) for d in range(ways)])  15 us
    add x1, other arithmetic, pair_terms(): first = sums[:, :, :, 0, :, 0] + sums[:, :, :, 1, :, 1]  14.1 us
    dynamic_slice x1, local copies, waits for them, and re-layouts, per_device(): own_cells = lax.dynamic_slice_in_dim(all_cells, first_date, local_dates, 0)  11.3 us
    concatenate x1, other arithmetic, per_device(): whole = jnp.roll(line, here * step, axis=0)  6.57 us
  transfers between devices with their start and end apart: 3, of which 3 were waited for; matrix products, arithmetic and copies ran while one was open for 0% of the time, Pallas kernels for 0%

profile of v1, /device:TPU:5, one launch (start us, length us, event | category | flops | bytes accessed | tf_op | source)
XLA Modules:
  0.0 220.7 jit_solution(1683710784332595914)
XLA Ops:
  0.0 1.2 collective-permute-start
  1.2 15.0 %collective-permute-done = bf16[10,2,12,1408]{3,1,2,0:T(2,128)(2,1)S(1)} collective-permute-done((bf16[10,2,12,1408]{3,1,2,0:T(2,128)(2,1)}, bf16[10,2,12,1408]{3,1,2,0:T(2,128)(2,1)S(1)}, u32[]{:S(2)}, u32[]{:S(2)}) %collective-permute-start) | collective-permute-done | bytes 675872 | tf_op jit(solution)/shard_map/ppermute | solution.py:63
  16.3 6.6 %fusion.9 = bf16[20,2,12,1408]{3,1,2,0:T(2,128)(2,1)S(1)} fusion(s32[]{:T(128)S(6)} %select_n.18, bf16[10,2,12,1408]{3,1,2,0:T(2,128)(2,1)S(1)} %collective-permute-done, bf16[10,2,12,1408]{3,1,2,0:T(2,128)(2,1)} %param.1), kind=kLoop, calls=%fused_computation.18 | loop fusion | flops 2027520 | bytes 2703364 | tf_op jit(solution)/shard_map/jit(_roll_dynamic)/concatenate | solution.py:67
  22.8 0.5 fusion.17
  23.3 4.6 %collective-permute-start.1 = (bf16[20,2,3,1408]{3,1,2,0:T(2,128)(2,1)S(1)}, bf16[20,2,3,1408]{3,1,2,0:T(2,128)(2,1)S(1)}, u32[]{:S(2)}, u32[]{:S(2)}) collective-permute-start(bf16[20,2,3,1408]{3,1,2,0:T(2,128)(2,1)S(1)} %get-tuple-element.9), channel_id=1, source_target_pairs={{0,1},{1,2},{2,3},{3,4},{4,5},{5,6},{6,7},{7,8},{8,9},{9,10},{10,1... | collective-permute-start | bytes 1013768 | tf_op jit(solution)/shard_map/ppermute | solution.py:17
  27.9 1.9 collective-permute-start.2
  29.8 2.2 collective-permute-done.1
  32.0 5.3 %collective-permute-done.2 = bf16[20,2,3,1408]{3,1,2,0:T(2,128)(2,1)S(1)} collective-permute-done((bf16[20,2,3,1408]{3,1,2,0:T(2,128)(2,1)S(1)}, bf16[20,2,3,1408]{3,1,2,0:T(2,128)(2,1)S(1)}, u32[]{:S(2)}, u32[]{:S(2)}) %collective-permute-start.2) | collective-permute-done | bytes 337952 | tf_op jit(solution)/shard_map/ppermute | solution.py:19
  37.3 6.8 %multiply_reduce_fusion = (f32[20,18,1408]{2,1,0:T(8,128)S(1)}, bf16[20,2,18,1408]{3,1,2,0:T(2,128)(2,1)}) fusion(bf16[20,2,3,1408]{3,1,2,0:T(2,128)(2,1)S(1)} %collective-permute-done.2, bf16[20,2,12,1408]{3,1,2,0:T(2,128)(2,1)S(1)} %fusion.9, bf16[20,2,3,1408]{3,1,2,0:T(2,128)(2,1)S(1)} %collective-permute-done.1), kind=kLoop, calls=%fused_computation.8 | loop fusion | flops 4561920 | bytes 6082560 | tf_op jit(solution)/shard_map/reduce_sum | solution.py:39
  44.1 0.4 copy.15
  44.5 26.0 %reduce_sum.14 = f32[20,6,3,128,11]{4,3,0,2,1:T(8,128)} reshape(f32[20,18,1408]{2,0,1:T(8,128)S(1)} %copy.15) | data formatting | bytes 4055040 | tf_op jit(solution)/shard_map/reduce_sum | solution.py:39
  70.5 9.4 %reduce_sum.18 = f32[20,6,128]{2,0,1:T(8,128)S(1)} reduce(f32[20,6,3,128,11]{4,3,0,2,1:T(8,128)} %reduce_sum.14, f32[]{:T(128)} %constant.32.clone.1), dimensions={2,4}, to_apply=%region_1.2 | reduce | flops 491520 | bytes 2088964 | tf_op jit(solution)/shard_map/reduce_sum | solution.py:39
  80.0 0.1 fusion.14
  80.2 0.0 copy-done
  80.2 54.0 %reshape.43 = bf16[20,2,6,3,128,11]{5,4,1,3,2,0:T(8,128)(2,1)} reshape(bf16[20,2,18,1408]{3,1,2,0:T(2,128)(2,1)S(1)} %copy-done) | data formatting | bytes 4055040 | tf_op jit(solution)/shard_map/reshape | solution.py:28
  134.2 11.3 %constant_dynamic-slice_fusion.1 = bf16[10,2,6,3,128,11]{5,4,1,3,2,0:T(8,128)(2,1)} fusion(bf16[20,2,6,3,128,11]{5,4,1,3,2,0:T(8,128)(2,1)} %reshape.43, s32[]{:T(128)S(6)} %select_n.19), kind=kLoop, calls=%fused_computation.35 | loop fusion | bytes 2027524 | tf_op jit(solution)/shard_map/dynamic_slice | solution.py:72
  145.5 45.5 %fusion.2 = f32[6,128,10,2,20,2]{4,2,5,3,1,0:T(8,128)} fusion(bf16[20,2,6,3,128,11,1]{5,4,1,3,2,0,6:T(8,128)(2,1)} %bitcast.21, bf16[10,2,6,3,128,11]{5,4,1,3,2,0:T(8,128)(2,1)} %constant_dynamic-slice_fusion.1), kind=kOutput, calls=%fused_computation.3 | convolution fusion | flops 40550400 | bytes 5498880 | tf_op jit(solution)/shard_map/dot_general | solution.py:44
  190.9 14.1 %fusion.6 = (f32[6,128,10,20,1]{3,2,1,0,4:T(8,128)}, f32[6,128,10,20,1]{3,2,1,0,4:T(8,128)}) fusion(f32[6,128,10,2,20,2]{4,2,5,3,1,0:T(8,128)} %fusion.2), kind=kLoop, calls=%fused_computation.7 | loop fusion | flops 307200 | bytes 3686400 | tf_op jit(solution)/shard_map/add | solution.py:50
  205.1 5.0 %copy.13 = f32[6,128,10,20,1]{1,4,3,2,0:T(1,128)S(1)} copy(f32[6,128,10,20,1]{3,2,1,0,4:T(8,128)} %get-tuple-element.7) | data formatting | bytes 1228800 | tf_op jit(solution)/shard_map/add | solution.py:50
  210.0 5.2 %copy.14 = f32[6,128,10,20,1]{1,4,3,2,0:T(1,128)S(1)} copy(f32[6,128,10,20,1]{3,2,1,0,4:T(8,128)} %get-tuple-element.8) | data formatting | bytes 1228800 | tf_op jit(solution)/shard_map/sub | solution.py:51
  215.2 1.1 maximum_bitcast_fusion
  216.4 2.6 %fusion.11 = f32[10,20,2,6,128]{4,2,1,0,3:T(2,128)S(1)} fusion(f32[10,20,2,6,128]{4,2,1,0,3:T(2,128)S(1)} %maximum_bitcast_fusion), kind=kLoop, calls=%fused_computation.20 | loop fusion | flops 614400 | bytes 2457600 | tf_op jit(solution)/shard_map/add | solution.py:33
  219.0 0.5 fusion.12
  219.5 1.2 copy.16
  (4 shorter events, 0.1 us)
Async XLA Ops:
  0.0 16.2 %collective-permute-start = (bf16[10,2,12,1408]{3,1,2,0:T(2,128)(2,1)}, bf16[10,2,12,1408]{3,1,2,0:T(2,128)(2,1)S(1)}, u32[]{:S(2)}, u32[]{:S(2)}) collective-permute-start(bf16[10,2,12,1408]{3,1,2,0:T(2,128)(2,1)} %param.1), channel_id=1, source_target_pairs={{0,16},{16,0},{1,17},{17,1},{2,18},{18,2},{3,19},{19,3},{4,20},{20... | collective-permute-start | bytes 2027528 | tf_op jit(solution)/shard_map/ppermute | solution.py:63
  23.3 8.7 %collective-permute-start.1 = (bf16[20,2,3,1408]{3,1,2,0:T(2,128)(2,1)S(1)}, bf16[20,2,3,1408]{3,1,2,0:T(2,128)(2,1)S(1)}, u32[]{:S(2)}, u32[]{:S(2)}) collective-permute-start(bf16[20,2,3,1408]{3,1,2,0:T(2,128)(2,1)S(1)} %get-tuple-element.9), channel_id=1, source_target_pairs={{0,1},{1,2},{2,3},{3,4},{4,5},{5,6},{6,7},{7,8},{8,9},{9,10},{10,1... | collective-permute-start | bytes 1013768 | tf_op jit(solution)/shard_map/ppermute | solution.py:17
  27.9 9.4 %collective-permute-start.2 = (bf16[20,2,3,1408]{3,1,2,0:T(2,128)(2,1)S(1)}, bf16[20,2,3,1408]{3,1,2,0:T(2,128)(2,1)S(1)}, u32[]{:S(2)}, u32[]{:S(2)}) collective-permute-start(bf16[20,2,3,1408]{3,1,2,0:T(2,128)(2,1)S(1)} %get-tuple-element.10), channel_id=1, source_target_pairs={{1,0},{2,1},{3,2},{4,3},{5,4},{6,5},{7,6},{8,7},{9,8},{10,9},{11,1... | collective-permute-start | bytes 1013768 | tf_op jit(solution)/shard_map/ppermute | solution.py:19
  70.5 9.6 %copy-start = (bf16[20,2,18,1408]{3,1,2,0:T(2,128)(2,1)S(1)}, bf16[20,2,18,1408]{3,1,2,0:T(2,128)(2,1)}, u32[]{:S(2)}) copy-start(bf16[20,2,18,1408]{3,1,2,0:T(2,128)(2,1)} %get-tuple-element.6) | copy-start | bytes 6082564
